TPU v7x, 512 devices: a whole 4x8x8 slice. The times are simulated.
512 devices in a mesh: src: 16 (over z, core), tgt: 32 (over x, y).
Axes of the slice: x: 4, y: 8, z: 8, core: 2. Of those that a mesh axis runs over, the one named last changes fastest.
Arguments:
- source_points: bfloat16 [32, 32768], P(None, 'src'), may hold values from -20 to 20
- target_points: bfloat16 [32, 32768], P(None, 'tgt'), may hold values from -20 to 20
- source_mass: float32 [32768], P('src'), may hold values from -1.5 to 1.5
- target_mass: float32 [32768], P('tgt'), may hold values from -1.5 to 1.5
- target_start: float32 [32768], P('tgt'), may hold values from -3 to 131
Outputs:
- source_potential: float32 [32768], P('src')
- target_potential: float32 [32768], P('tgt')
- mapped_cells: float32 [32, 32768], P(None, 'src')
All inputs are finite; a program needn't handle non-finite values.
Results may differ from a plain program's by a relative error of at most 0.0003.
Values sent between devices are 32-bit elements; how exact they have to be, the bound alone decides.
A program may use at most 64 MiB of HBM per device.

v0:
```python
import math

import jax
import jax.numpy as jnp
from jax import lax
from jax.sharding import PartitionSpec as P

ITERS = 2


entropic_blur = 0.5


def point_squares(points):
    return jnp.sum(jnp.square(points.astype(jnp.float32)), axis=0)


def pair_distances(points, squares, others, other_squares):
    inner_products = lax.dot_general(
        points, others, (((0,), (0,)), ((), ())), preferred_element_type=jnp.float32
    )
    return squares[:, None] + other_squares[None, :] - 2.0 * inner_products


def block_length(row_count):
    return max(row_count // 16, min(row_count, 128))


def row_partials(
    source_points, source_squares, target_points, target_squares, column_terms, with_values
):
    row_count = source_points.shape[1]
    block_rows = block_length(row_count)
    initial = [jnp.zeros((row_count,), jnp.float32), jnp.zeros((row_count,), jnp.float32)]
    if with_values:
        initial.append(jnp.zeros((target_points.shape[0], row_count), jnp.float32))

    def row_advance(turn_index, carried):
        offset = turn_index * block_rows
        source_piece = lax.dynamic_slice_in_dim(source_points, offset, block_rows, 1)
        piece_squares = lax.dynamic_slice_in_dim(source_squares, offset, block_rows, 0)
        scores = (
            column_terms[None, :]
            - pair_distances(source_piece, piece_squares, target_points, target_squares)
            / entropic_blur
        )
        maxima = jnp.max(scores, axis=1)
        weights = jnp.exp(scores - maxima[:, None])
        updated = [
            lax.dynamic_update_slice_in_dim(carried[0], maxima, offset, 0),
            lax.dynamic_update_slice_in_dim(carried[1], jnp.sum(weights, axis=1), offset, 0),
        ]
        if with_values:
            weighted = lax.dot_general(
                target_points,
                weights.astype(jnp.bfloat16),
                (((1,), (1,)), ((), ())),
                preferred_element_type=jnp.float32,
            )
            updated.append(lax.dynamic_update_slice_in_dim(carried[2], weighted, offset, 1))
        return tuple(updated)

    return lax.fori_loop(0, row_count // block_rows, row_advance, tuple(initial))


def column_partials(source_points, source_squares, row_terms, target_points, target_squares):
    row_count = source_points.shape[1]
    block_rows = block_length(row_count)
    columns = target_points.shape[1]
    initial = (jnp.full((columns,), -jnp.inf, jnp.float32), jnp.zeros((columns,), jnp.float32))

    def column_advance(turn_index, carried):
        offset = turn_index * block_rows
        source_piece = lax.dynamic_slice_in_dim(source_points, offset, block_rows, 1)
        piece_squares = lax.dynamic_slice_in_dim(source_squares, offset, block_rows, 0)
        piece_terms = lax.dynamic_slice_in_dim(row_terms, offset, block_rows, 0)
        scores = (
            piece_terms[:, None]
            - pair_distances(source_piece, piece_squares, target_points, target_squares)
            / entropic_blur
        )
        maxima = jnp.maximum(carried[0], jnp.max(scores, axis=0))
        totals = carried[1] * jnp.exp(carried[0] - maxima) + jnp.sum(
            jnp.exp(scores - maxima[None, :]), axis=0
        )
        return (maxima, totals)

    return lax.fori_loop(0, row_count // block_rows, column_advance, initial)


def source_update(maxima, totals):
    highest = lax.pmax(maxima, "tgt")
    masses = lax.psum(totals * jnp.exp(maxima - highest), "tgt")
    return -entropic_blur * (highest + jnp.log(masses))


def target_update(maxima, totals):
    highest = lax.pmax(maxima, "src")
    masses = lax.psum(totals * jnp.exp(maxima - highest), "src")
    return -entropic_blur * (highest + jnp.log(masses))


def mapped_update(maxima, totals, weighted):
    highest = lax.pmax(maxima, "tgt")
    scaling = jnp.exp(maxima - highest)
    masses, sums = lax.psum((totals * scaling, weighted * scaling[None, :]), "tgt")
    return sums / masses[None, :]


def local(source_points, target_points, source_mass, target_mass, target_start):
    source_squares = point_squares(source_points)
    target_squares = point_squares(target_points)
    source_terms = source_mass - math.log(source_points.shape[1] * lax.axis_size("src"))
    target_terms = target_mass - math.log(target_points.shape[1] * lax.axis_size("tgt"))
    target_potential = target_start
    source_potential = jnp.zeros_like(source_mass)
    for iteration in range(ITERS):
        maxima, totals = row_partials(
            source_points,
            source_squares,
            target_points,
            target_squares,
            target_potential / entropic_blur + target_terms,
            False,
        )
        source_potential = source_update(maxima, totals)
        maxima, totals = column_partials(
            source_points,
            source_squares,
            source_potential / entropic_blur + source_terms,
            target_points,
            target_squares,
        )
        target_potential = target_update(maxima, totals)
    maxima, totals, weighted = row_partials(
        source_points,
        source_squares,
        target_points,
        target_squares,
        target_potential / entropic_blur + target_terms,
        True,
    )
    return (source_potential, target_potential, mapped_update(maxima, totals, weighted))


def solution(mesh):
    placed = (P(None, "src"), P(None, "tgt"), P("src"), P("tgt"), P("tgt"))
    return jax.shard_map(
        local,
        mesh=mesh,
        in_specs=placed,
        out_specs=(P("src"), P("tgt"), P(None, "src")),
        check_vma=False,
    )
```

profile of v0, /device:TPU:6, one launch (start us, length us, event | category | flops | bytes accessed | tf_op | source)
XLA Modules:
  0.0 764.4 jit_solution(11235959706670379065)
XLA Ops:
  9.0 30.2 %while.79 = (s32[]{:T(128)}, f32[2048]{0:T(1024)S(1)}, f32[2048]{0:T(1024)S(1)}, f32[1024]{0:T(1024)S(1)}, f32[2048]{0:T(1024)S(1)}, /*index=5*/f32[1024]{0:T(10...) while((s32[]{:T(128)}, f32[2048]{0:T(1024)S(1)}, ...), condition=%wide.region_5.0_spmd, body=%wide.region_2.0_spmd.sunk | while | flops 9436934 | bytes 1135803 | solution.py:63
  9.1 1.1 fusion.61
  11.0 1.1 fusion.61
  12.9 1.1 fusion.61
  14.8 1.1 fusion.61
  16.7 1.1 fusion.61
  18.6 1.1 fusion.61
  20.5 1.1 fusion.61
  22.4 1.1 fusion.61
  24.3 1.1 fusion.61
  26.2 1.1 fusion.61
  28.1 1.1 fusion.61
  29.9 1.1 fusion.61
  31.8 1.1 fusion.61
  33.6 1.1 fusion.61
  35.5 1.1 fusion.61
  37.3 1.1 fusion.61
  39.1 64.7 %pmax.35 = f32[2048]{0:T(1024)S(1)} all-reduce(f32[2048]{0:T(1024)S(1)} %get-tuple-element.719), channel_id=1, replica_groups=mesh['src'=16,'tgt'=32] {'tgt'}, use_global_device_ids=true, to_apply=%region_6.0 | all-reduce | flops 2048 | bytes 16384 | tf_op jit(solution)/shard_map/pmax | solution.py:92
  103.9 70.6 %psum.42 = f32[2048]{0:T(1024)S(1)} all-reduce(f32[2048]{0:T(1024)S(1)} %exponential_multiply_fusion.1), channel_id=1, replica_groups=mesh['src'=16,'tgt'=32] {'tgt'}, use_global_device_ids=true, to_apply=%region_7.0 | all-reduce | flops 2048 | bytes 16384 | tf_op jit(solution)/shard_map/psum | solution.py:93
  174.5 20.9 %while.82 = (s32[]{:T(128)}, f32[1024]{0:T(1024)S(1)}, f32[1024]{0:T(1024)S(1)}, f32[2048]{0:T(1024)S(1)}, f32[2048]{0:T(1024)S(1)}, /*index=5*/f32[1024]{0:T(10...) while((s32[]{:T(128)}, f32[1024]{0:T(1024)S(1)}, ...), condition=%wide.region_11.0_spmd.clone, body=%wide.region_8.0_spmd.clone.sunk | while | flops 9442311 | bytes 1182914 | solution.py:88
  195.5 28.5 %pmax.36 = f32[1024]{0:T(1024)S(1)} all-reduce(f32[1024]{0:T(1024)S(1)} %get-tuple-element.721), channel_id=1, replica_groups=mesh['src'=16,'tgt'=32] {'src'}, use_global_device_ids=true, to_apply=%region_12.0 | all-reduce | flops 1024 | bytes 8192 | tf_op jit(solution)/shard_map/pmax | solution.py:98
  223.9 23.9 %psum.43 = f32[1024]{0:T(1024)S(1)} all-reduce(f32[1024]{0:T(1024)S(1)} %exponential_multiply_fusion.3), channel_id=1, replica_groups=mesh['src'=16,'tgt'=32] {'src'}, use_global_device_ids=true, to_apply=%region_13.0 | all-reduce | flops 1024 | bytes 8192 | tf_op jit(solution)/shard_map/psum | solution.py:99
  247.8 30.2 %while.80 = (s32[]{:T(128)}, f32[2048]{0:T(1024)S(1)}, f32[2048]{0:T(1024)S(1)}, f32[1024]{0:T(1024)S(1)}, f32[2048]{0:T(1024)S(1)}, /*index=5*/f32[1024]{0:T(10...) while((s32[]{:T(128)}, f32[2048]{0:T(1024)S(1)}, ...), condition=%wide.region_17.0_spmd, body=%wide.region_14.0_spmd.sunk | while | flops 9436934 | bytes 1135803 | solution.py:63
  247.9 1.1 fusion.63
  249.8 1.1 fusion.63
  251.8 1.1 fusion.63
  253.7 1.1 fusion.63
  255.6 1.1 fusion.63
  257.5 1.1 fusion.63
  259.4 1.1 fusion.63
  263.2 1.1 fusion.63
  265.1 1.1 fusion.63
  266.9 1.1 fusion.63
  268.8 1.1 fusion.63
  270.6 1.1 fusion.63
  272.5 1.1 fusion.63
  274.4 1.1 fusion.63
  276.2 1.1 fusion.63
  278.0 71.8 %pmax.37 = f32[2048]{0:T(1024)S(1)} all-reduce(f32[2048]{0:T(1024)S(1)} %get-tuple-element.723), channel_id=1, replica_groups=mesh['src'=16,'tgt'=32] {'tgt'}, use_global_device_ids=true, to_apply=%region_18.0 | all-reduce | flops 2048 | bytes 16384 | tf_op jit(solution)/shard_map/pmax | solution.py:92
  349.8 71.6 %psum.44 = f32[2048]{0:T(1024)S(1)} all-reduce(f32[2048]{0:T(1024)S(1)} %exponential_multiply_fusion), channel_id=1, replica_groups=mesh['src'=16,'tgt'=32] {'tgt'}, use_global_device_ids=true, to_apply=%region_19.0 | all-reduce | flops 2048 | bytes 16384 | tf_op jit(solution)/shard_map/psum | solution.py:93
  422.0 20.9 %while.83 = (s32[]{:T(128)}, f32[1024]{0:T(1024)S(1)}, f32[1024]{0:T(1024)S(1)}, f32[2048]{0:T(1024)S(1)}, f32[2048]{0:T(1024)S(1)}, /*index=5*/f32[1024]{0:T(10...) while((s32[]{:T(128)}, f32[1024]{0:T(1024)S(1)}, ...), condition=%wide.region_23.0_spmd.clone, body=%wide.region_20.0_spmd.clone.sunk | while | flops 9442311 | bytes 1182914 | solution.py:88
  442.9 23.6 %pmax.38 = f32[1024]{0:T(1024)S(1)} all-reduce(f32[1024]{0:T(1024)S(1)} %get-tuple-element.725), channel_id=1, replica_groups=mesh['src'=16,'tgt'=32] {'src'}, use_global_device_ids=true, to_apply=%region_24.0 | all-reduce | flops 1024 | bytes 8192 | tf_op jit(solution)/shard_map/pmax | solution.py:98
  466.5 23.5 %psum.45 = f32[1024]{0:T(1024)S(1)} all-reduce(f32[1024]{0:T(1024)S(1)} %exponential_multiply_fusion.2), channel_id=1, replica_groups=mesh['src'=16,'tgt'=32] {'src'}, use_global_device_ids=true, to_apply=%region_25.0 | all-reduce | flops 1024 | bytes 8192 | tf_op jit(solution)/shard_map/psum | solution.py:99
  490.7 34.7 %while.81 = (s32[]{:T(128)}, f32[2048]{0:T(1024)S(1)}, f32[2048]{0:T(1024)S(1)}, f32[32,2048]{1,0:T(8,128)S(1)}, f32[1024]{0:T(1024)S(1)}, /*index=5*/f32[2048]{...) while((s32[]{:T(128)}, f32[2048]{0:T(1024)S(1)}, ...), condition=%wide.region_29.0_spmd, body=%wide.region_26.0_spmd.sunk | while | flops 18087684 | bytes 1742535 | solution.py:63
  490.7 1.1 fusion.67
  492.9 1.1 fusion.67
  495.1 1.1 fusion.67
  497.3 1.1 fusion.67
  499.5 1.1 fusion.67
  501.7 1.1 fusion.67
  503.9 1.1 fusion.67
  506.1 1.1 fusion.67
  508.3 1.1 fusion.67
  510.4 1.1 fusion.67
  512.6 1.1 fusion.67
  514.7 1.1 fusion.67
  516.9 1.1 fusion.67
  519.0 1.1 fusion.67
  521.1 1.1 fusion.67
  523.3 1.1 fusion.67
  525.4 71.7 %pmax.39 = f32[2048]{0:T(1024)S(1)} all-reduce(f32[2048]{0:T(1024)S(1)} %get-tuple-element.728), channel_id=1, replica_groups=mesh['src'=16,'tgt'=32] {'tgt'}, use_global_device_ids=true, to_apply=%region_30.0 | all-reduce | flops 2048 | bytes 16384 | tf_op jit(solution)/shard_map/pmax | solution.py:104
  597.9 71.6 %psum.47 = f32[2048]{0:T(1024)S(1)} all-reduce(f32[2048]{0:T(1024)S(1)} %get-tuple-element.866), channel_id=1, replica_groups=mesh['src'=16,'tgt'=32] {'tgt'}, use_global_device_ids=true, to_apply=%region_32.0 | all-reduce | flops 2048 | bytes 16384 | tf_op jit(solution)/shard_map/psum | solution.py:106
  669.5 86.4 %all-reduce.2.cloned.1.call-done = f32[32,2048]{1,0:T(8,128)} async-done(((f32[32,2048]{1,0:T(8,128)}), f32[32,2048]{1,0:T(8,128)}) %all-reduce.2.cloned.1.call-update) | async-done | bytes 262160 | tf_op jit(solution)/shard_map/psum | solution.py:106
  755.9 1.7 broadcast_divide_fusion
  (467 shorter events, 88.9 us)
Async XLA Ops:
  7.2 748.8 %all-reduce.2.cloned.1.call-start = ((), (), s32[]{:S(2)}) async-start(), calls=%async_computation | async-start | bytes 524288 | tf_op jit(solution)/shard_map/psum | solution.py:106
  7.2 1.0 copy-start
  8.3 0.7 copy-start.1
  8.3 0.7 copy-start.3
  103.9 70.6 %copy-start.2 = (f32[2048]{0:T(1024)S(1)}, f32[2048]{0:T(1024)}, u32[]{:S(2)}) copy-start(f32[2048]{0:T(1024)} %param.17) | copy-start | bytes 24580
Sparse Core Ops, SparseCore 0:
  598.0 157.8 all-reduce.1
where the time goes:
time: 769 us; the launch traced here: 764 us
  blocking collectives  521 us (68%)
  matrix products  86.5 us (11%)
  waiting for transfers between devices  86.4 us (11%)
  local copies, waits for them, and re-layouts  34.7 us (5%)
  other arithmetic  19 us (2%)
  between operations  14.2 us (2%)
    psum x2, blocking collectives, source_update(): masses = lax.psum(totals * jnp.exp(maxima - highest), 'tgt')  142 us
    pmax x2, blocking collectives, source_update(): highest = lax.pmax(maxima, 'tgt')  136 us
    psum x1, waiting for transfers between devices, mapped_update(): lax.psum((totals * scaling, weighted * scaling[None, :]), 'tgt')  86.4 us
    dot_general x80, matrix products, pair_distances(): lax.dot_general(points, others, (((0,), (0,)), ((), ())), preferred_eleme...  82.1 us
    pmax x1, blocking collectives, mapped_update(): highest = lax.pmax(maxima, 'tgt')  71.7 us
    psum x1, blocking collectives, mapped_update(): lax.psum((totals * scaling, weighted * scaling[None, :]), 'tgt')  71.6 us
    pmax x2, blocking collectives, target_update(): highest = lax.pmax(maxima, 'src')  52 us
    psum x2, blocking collectives, target_update(): masses = lax.psum(totals * jnp.exp(maxima - highest), 'src')  47.4 us
  transfers between devices with their start and end apart: 1, of which 1 were waited for; matrix products, arithmetic and copies ran while one was open for 0% of the time, Pallas kernels for 0%

commit v1 on v0

v1 whole, which is shorter than its diff:
```python
import functools
import math

import jax
import jax.numpy as jnp
from jax import lax
from jax.experimental import pallas as pl
from jax.experimental.pallas import tpu as pltpu
from jax.sharding import PartitionSpec as P

ITERS = 2
MESH = pl.DeviceIdType.MESH
LOG2E = math.log2(math.e)
LN2 = math.log(2.0)
DEPTH = 128


def split3(value):
    high = value.astype(jnp.bfloat16).astype(jnp.float32)
    rest = value - high
    mid = rest.astype(jnp.bfloat16).astype(jnp.float32)
    return high, mid, rest - mid


def kernel(
    n_src, n_tgt, base,
    x_ref, y_ref, sm_ref, tm_ref, g0_ref,
    f_ref, g_ref, out_ref,
    xa, ya, xsq, ysq, fbuf, gbuf, vals, pieces,
    fsend, frecv, gsend, grecv, vsend, vrecv, osend, orecv,
):
    dim, rows = x_ref.shape
    columns = y_ref.shape[1]
    s = lax.axis_index("src")
    t = lax.axis_index("tgt")
    half = dim // 2
    width = 2 * rows // n_tgt

    barrier = pltpu.get_barrier_semaphore()

    def greet_tgt(d, carry):
        pl.semaphore_signal(
            barrier, inc=1, device_id={"tgt": lax.rem(t + d, n_tgt)}, device_id_type=MESH
        )
        return carry

    def greet_src(d, carry):
        pl.semaphore_signal(
            barrier, inc=1, device_id={"src": lax.rem(s + d, n_src)}, device_id_type=MESH
        )
        return carry

    lax.fori_loop(1, n_tgt, greet_tgt, 0)
    lax.fori_loop(1, n_src, greet_src, 0)

    x = x_ref[...].astype(jnp.float32)
    y = y_ref[...].astype(jnp.float32)
    xsq[...] = jnp.sum(x * x, axis=0, keepdims=True)
    ysq[...] = jnp.sum(y * y, axis=0, keepdims=True)
    for k, part in enumerate(split3(x * (4.0 * LOG2E))):
        xa[k * dim : (k + 1) * dim, :] = part.astype(jnp.bfloat16)
        ya[k * dim : (k + 1) * dim, :] = y_ref[...]
    xa[3 * dim :, :] = jnp.zeros((DEPTH - 3 * dim, rows), jnp.bfloat16)
    ya[3 * dim :, :] = jnp.zeros((DEPTH - 3 * dim, columns), jnp.bfloat16)

    def set_terms(ref, value):
        n = value.shape[1]
        row = lax.broadcasted_iota(jnp.int32, (16, n), 0)
        high, mid, low = split3(value)
        block = jnp.where(row == 0, high, jnp.where(row == 1, mid, jnp.where(row == 2, low, 0.0)))
        ref[3 * dim : 3 * dim + 16, :] = block.astype(jnp.bfloat16)

    def set_ones(ref):
        n = ref.shape[1]
        row = lax.broadcasted_iota(jnp.int32, (16, n), 0)
        ref[3 * dim : 3 * dim + 16, :] = jnp.where(row < 3, 1.0, 0.0).astype(jnp.bfloat16)

    def scores(left, right, offset, chunk):
        return lax.dot_general(
            left[...],
            right[:, pl.ds(offset, chunk)],
            (((0,), (0,)), ((), ())),
            preferred_element_type=jnp.float32,
        )

    def lse_pass(left, right, dst, chunk):
        n = right.shape[1]

        def advance(c, carry):
            offset = pl.multiple_of(c * chunk, chunk)
            block = scores(left, right, offset, chunk)
            top = jnp.max(block, axis=0, keepdims=True)
            total = jnp.sum(jnp.exp2(block - top), axis=0, keepdims=True)
            dst[:, pl.ds(offset, chunk)] = top + jnp.log2(total)
            return carry

        lax.fori_loop(0, n // chunk, advance, 0)

    def send_all(buf, me, axis, count, send, recv):
        def one(d, carry):
            pltpu.make_async_remote_copy(
                src_ref=buf.at[me],
                dst_ref=buf.at[me],
                send_sem=send,
                recv_sem=recv,
                device_id={axis: lax.rem(me + d, count)},
                device_id_type=MESH,
            ).start()
            return carry

        lax.fori_loop(1, count, one, 0)

    def whole(buf, count, axis, me, send, recv):
        part = buf.at[pl.ds(0, count - 1)]
        return pltpu.make_async_remote_copy(
            src_ref=part,
            dst_ref=part,
            send_sem=send,
            recv_sem=recv,
            device_id={axis: lax.rem(me + 1, count)},
            device_id_type=MESH,
        )

    def combine(buf):
        values = buf[...]
        top = jnp.max(values, axis=0)
        return top + jnp.log2(jnp.sum(jnp.exp2(values - top[None]), axis=0))

    column_terms = LOG2E * (2.0 * g0_ref[...] + tm_ref[...] - 2.0 * ysq[...]) - base
    for iteration in range(ITERS):
        set_terms(ya, column_terms)
        set_ones(xa)
        mine = fbuf.at[iteration]
        lse_pass(ya, xa, mine.at[t], 512)
        if iteration == 0:
            pl.semaphore_wait(barrier, n_src + n_tgt - 2)
        send_all(mine, t, "tgt", n_tgt, fsend.at[iteration], frecv.at[iteration])
        whole(mine, n_tgt, "tgt", t, fsend.at[iteration], frecv.at[iteration]).wait_recv()
        row_lse = combine(mine)
        if iteration == ITERS - 1:
            f_ref[...] = xsq[...] - (0.5 * LN2) * row_lse
        set_terms(xa, LOG2E * sm_ref[...] - base - row_lse)
        set_ones(ya)
        mine = gbuf.at[iteration]
        lse_pass(xa, ya, mine.at[s], 256)
        send_all(mine, s, "src", n_src, gsend.at[iteration], grecv.at[iteration])
        whole(mine, n_src, "src", s, gsend.at[iteration], grecv.at[iteration]).wait_recv()
        column_lse = combine(mine)
        if iteration == ITERS - 1:
            g_ref[...] = ysq[...] - (0.5 * LN2) * column_lse
        column_terms = LOG2E * tm_ref[...] - base - column_lse

    set_terms(ya, column_terms)
    set_ones(xa)
    chunk = 512

    def map_rows(c, carry):
        offset = pl.multiple_of(c * chunk, chunk)
        block = scores(ya, xa, offset, chunk)
        top = jnp.max(block, axis=0, keepdims=True)
        weights = jnp.exp2(block - top)
        total = jnp.sum(weights, axis=0, keepdims=True)
        summed = lax.dot_general(
            y_ref[...],
            weights.astype(jnp.bfloat16),
            (((1,), (0,)), ((), ())),
            preferred_element_type=jnp.float32,
        )
        mean = summed / total
        lse = jnp.broadcast_to(top + jnp.log2(total), (8, chunk))
        for h in range(2):
            vals[h, 0:half, pl.ds(offset, chunk)] = mean[h * half : (h + 1) * half]
            vals[h, half : half + 8, pl.ds(offset, chunk)] = lse
        return carry

    lax.fori_loop(0, rows // chunk, map_rows, 0)

    def column_of(p):
        return pl.multiple_of((p // 2) * width, width)

    def send_piece(d, carry):
        p = lax.rem(t + d, n_tgt)
        pltpu.make_async_remote_copy(
            src_ref=vals.at[lax.rem(p, 2), :, pl.ds(column_of(p), width)],
            dst_ref=pieces.at[t],
            send_sem=vsend,
            recv_sem=vrecv,
            device_id={"tgt": p},
            device_id_type=MESH,
        ).start()
        return carry

    lax.fori_loop(1, n_tgt, send_piece, 0)
    pieces[t] = vals[lax.rem(t, 2), :, pl.ds(column_of(t), width)]
    whole(pieces, n_tgt, "tgt", t, vsend, vrecv).wait_recv()
    lse = pieces[:, half : half + 1, :]
    top = jnp.max(lse, axis=0, keepdims=True)
    share = jnp.exp2(lse - top)
    image = jnp.sum(pieces[:, 0:half, :] * share, axis=0) / jnp.sum(share, axis=0)
    spot = (pl.ds(pl.multiple_of(lax.rem(t, 2) * half, half), half), pl.ds(column_of(t), width))
    out_ref[spot] = image

    def send_image(d, carry):
        pltpu.make_async_remote_copy(
            src_ref=out_ref.at[spot],
            dst_ref=out_ref.at[spot],
            send_sem=osend,
            recv_sem=orecv,
            device_id={"tgt": lax.rem(t + d, n_tgt)},
            device_id_type=MESH,
        ).start()
        return carry

    lax.fori_loop(1, n_tgt, send_image, 0)

    def all_images():
        part = pieces.at[pl.ds(0, n_tgt - 1), 0:half, :]
        return pltpu.make_async_remote_copy(
            src_ref=part,
            dst_ref=part,
            send_sem=osend,
            recv_sem=orecv,
            device_id={"tgt": lax.rem(t + 1, n_tgt)},
            device_id_type=MESH,
        )

    all_images().wait_recv()
    for iteration in range(ITERS):
        whole(fbuf.at[iteration], n_tgt, "tgt", t, fsend.at[iteration], frecv.at[iteration]).wait_send()
        whole(gbuf.at[iteration], n_src, "src", s, gsend.at[iteration], grecv.at[iteration]).wait_send()
    whole(pieces, n_tgt, "tgt", t, vsend, vrecv).wait_send()
    all_images().wait_send()


def solution(mesh):
    n_src, n_tgt = mesh.shape["src"], mesh.shape["tgt"]

    def local(source_points, target_points, source_mass, target_mass, target_start):
        dim, rows = source_points.shape
        columns = target_points.shape[1]
        f32 = jnp.float32
        vmem = pl.BlockSpec(memory_space=pltpu.VMEM)
        dma = pltpu.SemaphoreType.DMA
        f, g, mapped = pl.pallas_call(
            functools.partial(kernel, n_src, n_tgt, math.log2(rows * n_src)),
            out_shape=(
                jax.ShapeDtypeStruct((1, rows), f32),
                jax.ShapeDtypeStruct((1, columns), f32),
                jax.ShapeDtypeStruct((dim, rows), f32),
            ),
            in_specs=[vmem] * 5,
            out_specs=(vmem,) * 3,
            scratch_shapes=[
                pltpu.VMEM((DEPTH, rows), jnp.bfloat16),
                pltpu.VMEM((DEPTH, columns), jnp.bfloat16),
                pltpu.VMEM((1, rows), f32),
                pltpu.VMEM((1, columns), f32),
                pltpu.VMEM((ITERS, n_tgt, 1, rows), f32),
                pltpu.VMEM((ITERS, n_src, 1, columns), f32),
                pltpu.VMEM((2, dim // 2 + 8, rows), f32),
                pltpu.VMEM((n_tgt, dim // 2 + 8, 2 * rows // n_tgt), f32),
                dma((ITERS,)),
                dma((ITERS,)),
                dma((ITERS,)),
                dma((ITERS,)),
                dma,
                dma,
                dma,
                dma,
            ],
            compiler_params=pltpu.CompilerParams(
                collective_id=0, has_side_effects=True, vmem_limit_bytes=50 << 20
            ),
        )(
            source_points,
            target_points,
            source_mass.reshape(1, rows),
            target_mass.reshape(1, columns),
            target_start.reshape(1, columns),
        )
        return f.reshape(rows), g.reshape(columns), mapped

    placed = (P(None, "src"), P(None, "tgt"), P("src"), P("tgt"), P("tgt"))
    return jax.shard_map(
        local,
        mesh=mesh,
        in_specs=placed,
        out_specs=(P("src"), P("tgt"), P(None, "src")),
        check_vma=False,
    )
```

time: 769 us -> 86.5 us (0.11)
  blocking collectives: 521 us -> 0 us
  matrix products: 86.5 us -> 0 us
  waiting for transfers between devices: 86.4 us -> 0 us
  Pallas kernels: 0 us -> 78.8 us
  local copies, waits for them, and re-layouts: 34.7 us -> 5.7 us
  other arithmetic: 19 us -> 0 us
  between operations: 14.2 us -> 0.65 us
    psum x5 -> x0, blocking collectives: 261 us -> none  [the longest x2 142 us: source_update(): masses = lax.psum(totals * jnp.exp(maxima - highest), 'tgt')]
    pmax x5 -> x0, blocking collectives: 260 us -> none  [the longest x2 136 us: source_update(): highest = lax.pmax(maxima, 'tgt')]
    dot_general x96 -> x0, matrix products: 86.5 us -> none  [the longest x80 82.1 us: pair_distances(): lax.dot_general(points, others, (((0,), (0,)), ((), ())), preferred_eleme...]
    psum x1 -> x0, waiting for transfers between devices: 86.4 us -> none  [mapped_update(): lax.psum((totals * scaling, weighted * scaling[None, :]), 'tgt')]
    pallas_call x0 -> x1, Pallas kernels: none -> 78.8 us  [local(): pl.pallas_call(functools.partial(kernel, n_src, n_tgt, math.log2(rows * n...]
    dynamic_update_slice x96 -> x0, local copies, waits for them, and re-layouts: 25.4 us -> none  [the longest x48 12.7 us: row_advance(): lax.dynamic_update_slice_in_dim(carried[1], jnp.sum(weights, axis=1), off...]
    reduce_sum x82 -> x0, other arithmetic: 14.7 us -> none  [the longest x48 10.7 us: row_advance(): jnp.sum(weights, axis=1)]
    dynamic_slice x112 -> x0, local copies, waits for them, and re-layouts: 8.53 us -> none  [the longest x48 3.67 us: row_advance(): lax.dynamic_slice_in_dim(source_squares, offset, block_rows, 0)]
  transfers between devices with their start and end apart: 1 -> 0, of which waited for: 1 -> 0; matrix products, arithmetic and copies ran while one was open for 0% -> 0% of each run, Pallas kernels for 0% -> 0%
where the time goes in v1:
time: 86.5 us; the launch traced here: 85.2 us
  Pallas kernels  78.8 us (91%)
  local copies, waits for them, and re-layouts  5.7 us (7%)
    pallas_call x1, Pallas kernels, local(): pl.pallas_call(functools.partial(kernel, n_src, n_tgt, math.log2(rows * n...  78.8 us
    unnamed x13, local copies, waits for them, and re-layouts  5.7 us

profile of v1, /device:TPU:6, one launch (start us, length us, event | category | flops | bytes accessed | tf_op | source)
XLA Modules:
  0.0 85.2 jit_solution(14145679339439867694)
XLA Ops:
  0.6 0.0 copy-start.3
  0.6 0.7 copy-done.3
  1.3 0.0 copy-start
  1.3 0.9 %copy-done = bf16[32,2048]{1,0:T(8,128)(2,1)S(1)} copy-done((bf16[32,2048]{1,0:T(8,128)(2,1)S(1)}, bf16[32,2048]{1,0:T(8,128)(2,1)}, u32[]{:S(2)}) %copy-start) | copy-done | bytes 131096
  2.2 0.0 copy-start.1
  2.2 0.8 copy-done.1
  3.1 0.0 copy-start.2
  3.1 0.7 copy-done.2
  3.8 0.0 copy-start.4
  3.8 0.7 copy-done.4
  4.4 78.8 %shard_map.76 = (f32[1,2048]{1,0:T(1,128)S(1)}, f32[1,1024]{1,0:T(1,128)S(1)}, f32[32,2048]{1,0:T(8,128)S(1)}) custom-call(bf16[32,2048]{1,0:T(8,128)(2,1)S(1)} %copy-done, bf16[32,1024]{1,0:T(8,128)(2,1)S(1)} %copy-done.1, f32[1,2048]{1,0:T(1,128)S(1)} %bitcast.6, f32[1,1024]{1,0:T(1,128)S(1)} %bitcast.8, f32[1,1024]{1,0:T(1,128)S(1)} %bitcast.9), custom_call_target="tpu_custom_call" | custom-call | tf_op jit(solution)/shard_map/pallas_call | solution.py:244
  83.3 0.6 copy.11
  83.9 0.6 copy.12
  84.5 0.7 copy.13
Async XLA Ops:
  0.6 0.7 copy-start.3
  1.3 0.9 %copy-start = (bf16[32,2048]{1,0:T(8,128)(2,1)S(1)}, bf16[32,2048]{1,0:T(8,128)(2,1)}, u32[]{:S(2)}) copy-start(bf16[32,2048]{1,0:T(8,128)(2,1)} %x_ref.1) | copy-start | bytes 393220
  2.2 0.8 copy-start.1
  3.1 0.7 copy-start.2
  3.8 0.7 copy-start.4

commit v2 on v1

v2 whole, which is shorter than its diff:
```python
import functools
import math

import jax
import jax.numpy as jnp
from jax import lax
from jax.experimental import pallas as pl
from jax.experimental.pallas import tpu as pltpu
from jax.sharding import PartitionSpec as P

ITERS = 2
MESH = pl.DeviceIdType.MESH
LOG2E = math.log2(math.e)
LN2 = math.log(2.0)
DEPTH = 128
CHUNKS = 4
HALVES = 2


def split3(value):
    high = value.astype(jnp.bfloat16).astype(jnp.float32)
    rest = value - high
    mid = rest.astype(jnp.bfloat16).astype(jnp.float32)
    return high, mid, rest - mid


def term_rows(value):
    n = value.shape[1]
    row = lax.broadcasted_iota(jnp.int32, (16, n), 0)
    high, mid, low = split3(value)
    block = jnp.where(row == 0, high, jnp.where(row == 1, mid, jnp.where(row == 2, low, 0.0)))
    return block.astype(jnp.bfloat16)


def one_rows(n):
    row = lax.broadcasted_iota(jnp.int32, (16, n), 0)
    return jnp.where(row < 3, 1.0, 0.0).astype(jnp.bfloat16)


def combine(values):
    top = jnp.max(values, axis=0)
    return top + jnp.log2(jnp.sum(jnp.exp2(values - top[None]), axis=0))


def scores(left, right):
    return lax.dot_general(
        left, right, (((0,), (0,)), ((), ())), preferred_element_type=jnp.float32
    )


def partial(block):
    n = block.shape[1]
    groups = block.reshape(block.shape[0] // 8, 8, n)
    top = jnp.max(groups, axis=0)
    return top, jnp.sum(jnp.exp2(groups - top[None]), axis=0)


def merge(first, second):
    top = jnp.maximum(first[0], second[0])
    return top, first[1] * jnp.exp2(first[0] - top) + second[1] * jnp.exp2(second[0] - top)


def finish(pair):
    top = jnp.max(pair[0], axis=0, keepdims=True)
    return top + jnp.log2(jnp.sum(pair[1] * jnp.exp2(pair[0] - top), axis=0, keepdims=True))


def kernel(
    n_src, n_tgt, src_base, tgt_base,
    x_hbm, y_hbm, sm_hbm, tm_hbm, g0_hbm,
    f_ref, g_ref, out_ref,
    x_ref, y_ref, sm_ref, tm_ref, g0_ref,
    xr, xc, yr, yc, xsq, ysq, rtop, rsum, ctop, csum, fbuf, gbuf, vals, pieces,
    loads, fsend, frecv, gsend, grecv, vsend, vrecv, osend, orecv,
):
    dim, rows = x_ref.shape
    columns = y_ref.shape[1]
    s = lax.axis_index("src")
    t = lax.axis_index("tgt")
    half = dim // 2
    width = 2 * rows // n_tgt
    chunk = rows // CHUNKS
    span = columns // HALVES

    copies = [
        pltpu.make_async_copy(a, b, loads.at[k])
        for k, (a, b) in enumerate(
            (
                (x_hbm, x_ref),
                (y_hbm, y_ref),
                (sm_hbm, sm_ref),
                (tm_hbm, tm_ref),
                (g0_hbm, g0_ref),
            )
        )
    ]
    for copy in copies:
        copy.start()

    barrier = pltpu.get_barrier_semaphore()

    def greet_tgt(d, carry):
        pl.semaphore_signal(
            barrier, inc=1, device_id={"tgt": lax.rem(t + d, n_tgt)}, device_id_type=MESH
        )
        return carry

    def greet_src(d, carry):
        pl.semaphore_signal(
            barrier, inc=1, device_id={"src": lax.rem(s + d, n_src)}, device_id_type=MESH
        )
        return carry

    lax.fori_loop(1, n_tgt, greet_tgt, 0)
    lax.fori_loop(1, n_src, greet_src, 0)
    for copy in copies:
        copy.wait()

    x = x_ref[...].astype(jnp.float32)
    y = y_ref[...].astype(jnp.float32)
    xsq[...] = jnp.sum(x * x, axis=0, keepdims=True)
    ysq[...] = jnp.sum(y * y, axis=0, keepdims=True)
    for k, part in enumerate(split3(x * (4.0 * LOG2E))):
        rounded = part.astype(jnp.bfloat16)
        at = slice(k * dim, (k + 1) * dim)
        xr[at, :] = rounded
        xc[at, :] = rounded
        yr[at, :] = y_ref[...]
        yc[at, :] = y_ref[...]
    used = 3 * dim
    extra = slice(used, used + 16)
    for ref in (xr, xc, yr, yc):
        ref[used:, :] = jnp.zeros((DEPTH - used, ref.shape[1]), jnp.bfloat16)
    xr[extra, :] = one_rows(rows)
    yc[extra, :] = one_rows(columns)

    def send_all(buf, me, axis, count, send, recv):
        def one(d, carry):
            pltpu.make_async_remote_copy(
                src_ref=buf.at[me],
                dst_ref=buf.at[me],
                send_sem=send,
                recv_sem=recv,
                device_id={axis: lax.rem(me + d, count)},
                device_id_type=MESH,
            ).start()
            return carry

        lax.fori_loop(1, count, one, 0)

    def whole(buf, count, axis, me, send, recv):
        part = buf.at[pl.ds(0, count - 1)]
        return pltpu.make_async_remote_copy(
            src_ref=part,
            dst_ref=part,
            send_sem=send,
            recv_sem=recv,
            device_id={axis: lax.rem(me + 1, count)},
            device_id_type=MESH,
        )

    def f_all(i, c):
        return whole(fbuf.at[i, c], n_tgt, "tgt", t, fsend.at[i, c], frecv.at[i, c])

    def g_all(i, h):
        return whole(gbuf.at[i, h], n_src, "src", s, gsend.at[i, h], grecv.at[i, h])

    for iteration in range(ITERS):
        for h in range(HALVES):
            cols = slice(h * span, (h + 1) * span)
            if iteration == 0:
                terms = (
                    LOG2E * (2.0 * g0_ref[:, cols] + tm_ref[:, cols] - 2.0 * ysq[:, cols])
                    - tgt_base
                )
            else:
                g_all(iteration - 1, h).wait_recv()
                terms = LOG2E * tm_ref[:, cols] - tgt_base - combine(gbuf[iteration - 1, h])
            yr[extra, cols] = term_rows(terms)
            for c in range(CHUNKS):
                at = slice(c * chunk, (c + 1) * chunk)
                pair = partial(scores(yr[:, cols], xr[:, at]))
                if h > 0:
                    pair = merge((rtop[:, at], rsum[:, at]), pair)
                if h < HALVES - 1:
                    rtop[:, at], rsum[:, at] = pair
                else:
                    fbuf[iteration, c, t] = finish(pair)
                    if iteration > 0:
                        send_all(
                            fbuf.at[iteration, c], t, "tgt", n_tgt,
                            fsend.at[iteration, c], frecv.at[iteration, c],
                        )
        if iteration == 0:
            pl.semaphore_wait(barrier, n_src + n_tgt - 2)
            for c in range(CHUNKS):
                send_all(
                    fbuf.at[iteration, c], t, "tgt", n_tgt,
                    fsend.at[iteration, c], frecv.at[iteration, c],
                )
        for c in range(CHUNKS):
            at = slice(c * chunk, (c + 1) * chunk)
            f_all(iteration, c).wait_recv()
            row_lse = combine(fbuf[iteration, c])
            if iteration == ITERS - 1:
                f_ref[:, at] = xsq[:, at] - (0.5 * LN2) * row_lse
            xc[extra, at] = term_rows(LOG2E * sm_ref[:, at] - src_base - row_lse)
            for h in range(HALVES):
                cols = slice(h * span, (h + 1) * span)
                pair = partial(scores(xc[:, at], yc[:, cols]))
                if c > 0:
                    pair = merge((ctop[:, cols], csum[:, cols]), pair)
                if c < CHUNKS - 1:
                    ctop[:, cols], csum[:, cols] = pair
                else:
                    gbuf[iteration, h, s] = finish(pair)
                    send_all(
                        gbuf.at[iteration, h], s, "src", n_src,
                        gsend.at[iteration, h], grecv.at[iteration, h],
                    )

    for h in range(HALVES):
        cols = slice(h * span, (h + 1) * span)
        g_all(ITERS - 1, h).wait_recv()
        column_lse = combine(gbuf[ITERS - 1, h])
        g_ref[:, cols] = ysq[:, cols] - (0.5 * LN2) * column_lse
        yr[extra, cols] = term_rows(LOG2E * tm_ref[:, cols] - tgt_base - column_lse)

    def send_piece(d, first):
        p = first + d

        @pl.when(p != t)
        def _():
            pltpu.make_async_remote_copy(
                src_ref=vals.at[lax.rem(p, 2), :, pl.ds(column_of(p), width)],
                dst_ref=pieces.at[t],
                send_sem=vsend,
                recv_sem=vrecv,
                device_id={"tgt": p},
                device_id_type=MESH,
            ).start()

        return first

    def column_of(p):
        return pl.multiple_of((p // 2) * width, width)

    owners = n_tgt // CHUNKS
    for turn in (2, 1, 3, 0):
        c = lax.rem(t // owners + turn, CHUNKS)
        at = pl.ds(pl.multiple_of(c * chunk, chunk), chunk)
        block = scores(yr[...], xr[:, at])
        top = jnp.max(block, axis=0, keepdims=True)
        weights = jnp.exp2(block - top)
        total = jnp.sum(weights, axis=0, keepdims=True)
        summed = lax.dot_general(
            y_ref[...],
            weights.astype(jnp.bfloat16),
            (((1,), (0,)), ((), ())),
            preferred_element_type=jnp.float32,
        )
        mean = summed / total
        lse = jnp.broadcast_to(top + jnp.log2(total), (8, chunk))
        for k in range(2):
            vals[k, 0:half, at] = mean[k * half : (k + 1) * half]
            vals[k, half : half + 8, at] = lse
        lax.fori_loop(0, owners, send_piece, c * owners)

    pieces[t] = vals[lax.rem(t, 2), :, pl.ds(column_of(t), width)]
    whole(pieces, n_tgt, "tgt", t, vsend, vrecv).wait_recv()
    lse = pieces[:, half : half + 1, :]
    top = jnp.max(lse, axis=0, keepdims=True)
    share = jnp.exp2(lse - top)
    image = jnp.sum(pieces[:, 0:half, :] * share, axis=0) / jnp.sum(share, axis=0)
    spot = (pl.ds(pl.multiple_of(lax.rem(t, 2) * half, half), half), pl.ds(column_of(t), width))
    out_ref[spot] = image

    def send_image(d, carry):
        pltpu.make_async_remote_copy(
            src_ref=out_ref.at[spot],
            dst_ref=out_ref.at[spot],
            send_sem=osend,
            recv_sem=orecv,
            device_id={"tgt": lax.rem(t + d, n_tgt)},
            device_id_type=MESH,
        ).start()
        return carry

    lax.fori_loop(1, n_tgt, send_image, 0)

    def all_images():
        part = pieces.at[pl.ds(0, n_tgt - 1), 0:half, :]
        return pltpu.make_async_remote_copy(
            src_ref=part,
            dst_ref=part,
            send_sem=osend,
            recv_sem=orecv,
            device_id={"tgt": lax.rem(t + 1, n_tgt)},
            device_id_type=MESH,
        )

    for iteration in range(ITERS):
        for c in range(CHUNKS):
            f_all(iteration, c).wait_send()
        for h in range(HALVES):
            g_all(iteration, h).wait_send()
    whole(pieces, n_tgt, "tgt", t, vsend, vrecv).wait_send()
    all_images().wait_recv()
    all_images().wait_send()


def store(f_in, g_in, out_in, f_out, g_out, out_out, sems):
    copies = [
        pltpu.make_async_copy(a, b, sems.at[k])
        for k, (a, b) in enumerate(((out_in, out_out), (f_in, f_out), (g_in, g_out)))
    ]
    for copy in copies:
        copy.start()
    for copy in copies:
        copy.wait()


def solution(mesh):
    n_src, n_tgt = mesh.shape["src"], mesh.shape["tgt"]

    def local(source_points, target_points, source_mass, target_mass, target_start):
        dim, rows = source_points.shape
        columns = target_points.shape[1]
        f32, bf16 = jnp.float32, jnp.bfloat16
        vmem = pl.BlockSpec(memory_space=pltpu.VMEM)
        hbm = pl.BlockSpec(memory_space=pltpu.HBM)
        dma = pltpu.SemaphoreType.DMA
        outs = (
            jax.ShapeDtypeStruct((1, rows), f32),
            jax.ShapeDtypeStruct((1, columns), f32),
            jax.ShapeDtypeStruct((dim, rows), f32),
        )
        chunk, span = rows // CHUNKS, columns // HALVES
        results = pl.pallas_call(
            functools.partial(
                kernel, n_src, n_tgt, math.log2(rows * n_src), math.log2(columns * n_tgt)
            ),
            out_shape=outs,
            in_specs=[hbm] * 5,
            out_specs=(vmem,) * 3,
            scratch_shapes=[
                pltpu.VMEM((dim, rows), bf16),
                pltpu.VMEM((dim, columns), bf16),
                pltpu.VMEM((1, rows), f32),
                pltpu.VMEM((1, columns), f32),
                pltpu.VMEM((1, columns), f32),
                pltpu.VMEM((DEPTH, rows), bf16),
                pltpu.VMEM((DEPTH, rows), bf16),
                pltpu.VMEM((DEPTH, columns), bf16),
                pltpu.VMEM((DEPTH, columns), bf16),
                pltpu.VMEM((1, rows), f32),
                pltpu.VMEM((1, columns), f32),
                pltpu.VMEM((8, rows), f32),
                pltpu.VMEM((8, rows), f32),
                pltpu.VMEM((8, columns), f32),
                pltpu.VMEM((8, columns), f32),
                pltpu.VMEM((ITERS, CHUNKS, n_tgt, 1, chunk), f32),
                pltpu.VMEM((ITERS, HALVES, n_src, 1, span), f32),
                pltpu.VMEM((2, dim // 2 + 8, rows), f32),
                pltpu.VMEM((n_tgt, dim // 2 + 8, 2 * rows // n_tgt), f32),
                dma((5,)),
                dma((ITERS, CHUNKS)),
                dma((ITERS, CHUNKS)),
                dma((ITERS, HALVES)),
                dma((ITERS, HALVES)),
                dma,
                dma,
                dma,
                dma,
            ],
            compiler_params=pltpu.CompilerParams(
                collective_id=0, has_side_effects=True, vmem_limit_bytes=48 << 20
            ),
        )(
            *[pltpu.with_memory_space_constraint(v, pltpu.HBM) for v in (source_points, target_points, source_mass.reshape(1, rows), target_mass.reshape(1, columns), target_start.reshape(1, columns))]
        )
        f, g, mapped = pl.pallas_call(
            store,
            out_shape=outs,
            in_specs=[vmem] * 3,
            out_specs=(hbm,) * 3,
            scratch_shapes=[dma((3,))],
            compiler_params=pltpu.CompilerParams(vmem_limit_bytes=1 << 20),
        )(*results)
        return f.reshape(rows), g.reshape(columns), mapped

    placed = (P(None, "src"), P(None, "tgt"), P("src"), P("tgt"), P("tgt"))
    return jax.shard_map(
        local,
        mesh=mesh,
        in_specs=placed,
        out_specs=(P("src"), P("tgt"), P(None, "src")),
        check_vma=False,
    )
```

time: 86.5 us -> 71.5 us (0.83)
  Pallas kernels: 78.8 us -> 70.1 us
  local copies, waits for them, and re-layouts: 5.7 us -> 0 us
    pallas_call x1, Pallas kernels: 78.8 us -> 69.4 us  [local(): pl.pallas_call(functools.partial(kernel, n_src, n_tgt, math.log2(rows * n...]
    unnamed x13 -> x0, local copies, waits for them, and re-layouts: 5.7 us -> none
where the time goes in v2:
time: 71.5 us; the launch traced here: 70.7 us
  Pallas kernels  70.1 us (98%)
    pallas_call x1, Pallas kernels, local(): pl.pallas_call(functools.partial(kernel, n_src, n_tgt, math.log2(rows * n...  69.4 us

profile of v2, /device:TPU:6, one launch (start us, length us, event | category | flops | bytes accessed | tf_op | source)
XLA Modules:
  0.0 70.7 jit_solution(18243568072223738995)
XLA Ops:
  0.6 69.4 %shard_map.76 = (f32[1,2048]{1,0:T(1,128)S(1)}, f32[1,1024]{1,0:T(1,128)S(1)}, f32[32,2048]{1,0:T(8,128)S(1)}) custom-call(bf16[32,2048]{1,0:T(8,128)(2,1)} %x_hbm.1, bf16[32,1024]{1,0:T(8,128)(2,1)} %y_hbm.1, f32[1,2048]{1,0:T(1,128)} %bitcast.5, f32[1,1024]{1,0:T(1,128)} %bitcast.6, f32[1,1024]{1,0:T(1,128)} %bitcast.7), custom_call_target="tpu_custom_call" | custom-call | tf_op jit(solution)/shard_map/pallas_call | solution.py:339
  70.0 0.7 %shard_map.77 = (f32[1,2048]{1,0:T(1,128)}, f32[1,1024]{1,0:T(1,128)}, f32[32,2048]{1,0:T(8,128)}) custom-call(f32[1,2048]{1,0:T(1,128)S(1)} %get-tuple-element.9.f_in, f32[1,1024]{1,0:T(1,128)S(1)} %get-tuple-element.10.g_in, f32[32,2048]{1,0:T(8,128)S(1)} %get-tuple-element.11.out_in), custom_call_target="tpu_custom_call" | custom-call | tf_op jit(solution)/shard_map/pallas_call | solution.py:382

commit v3 on v2

--- a/solution.py
+++ b/solution.py
@@ -14,7 +14,12 @@
 LN2 = math.log(2.0)
 DEPTH = 128
 CHUNKS = 4
-HALVES = 2
+HALVES = 1
+PHASES = 2
+
+
+def far_first(n):
+    return sorted(range(n), key=lambda d: -min(d, n - d))
 
 
 def split3(value):
@@ -70,15 +75,15 @@
     x_hbm, y_hbm, sm_hbm, tm_hbm, g0_hbm,
     f_ref, g_ref, out_ref,
     x_ref, y_ref, sm_ref, tm_ref, g0_ref,
-    xr, xc, yr, yc, xsq, ysq, rtop, rsum, ctop, csum, fbuf, gbuf, vals, pieces,
-    loads, fsend, frecv, gsend, grecv, vsend, vrecv, osend, orecv,
+    xr, xc, yr, yc, xsq, ysq, rtop, rsum, ctop, csum, fbuf, gbuf, vals, logs, pieces, shares,
+    loads, fsend, frecv, gsend, grecv, vsend, vrecv, lsend, lrecv, osend, orecv,
 ):
     dim, rows = x_ref.shape
     columns = y_ref.shape[1]
     s = lax.axis_index("src")
     t = lax.axis_index("tgt")
-    half = dim // 2
-    width = 2 * rows // n_tgt
+    groups = dim // 8
+    width = groups * rows // (PHASES * n_tgt)
     chunk = rows // CHUNKS
     span = columns // HALVES
 
@@ -97,22 +102,18 @@
     for copy in copies:
         copy.start()
 
+    nx, ny, nz = 4, n_tgt // 4, n_src // 2
+    xs = [lax.rem(t // ny + d, nx) * ny for d in far_first(nx)]
+    ys = [lax.rem(lax.rem(t, ny) + d, ny) for d in far_first(ny)]
+    zs = [lax.rem(s // 2 + d, nz) * 2 for d in far_first(nz)]
+    cs = [1 - lax.rem(s, 2), lax.rem(s, 2)]
+    tgt_peers = [b + a for a in ys for b in xs][:-1]
+    src_peers = [b + a for b in zs for a in cs][:-1]
+
     barrier = pltpu.get_barrier_semaphore()
-
-    def greet_tgt(d, carry):
-        pl.semaphore_signal(
-            barrier, inc=1, device_id={"tgt": lax.rem(t + d, n_tgt)}, device_id_type=MESH
-        )
-        return carry
-
-    def greet_src(d, carry):
-        pl.semaphore_signal(
-            barrier, inc=1, device_id={"src": lax.rem(s + d, n_src)}, device_id_type=MESH
-        )
-        return carry
-
-    lax.fori_loop(1, n_tgt, greet_tgt, 0)
-    lax.fori_loop(1, n_src, greet_src, 0)
+    for axis, peers in (("tgt", tgt_peers), ("src", src_peers)):
+        for peer in peers:
+            pl.semaphore_signal(barrier, inc=1, device_id={axis: peer}, device_id_type=MESH)
     for copy in copies:
         copy.wait()
 
@@ -135,18 +136,15 @@
     yc[extra, :] = one_rows(columns)
 
     def send_all(buf, me, axis, count, send, recv):
-        def one(d, carry):
+        for peer in tgt_peers if axis == "tgt" else src_peers:
             pltpu.make_async_remote_copy(
                 src_ref=buf.at[me],
                 dst_ref=buf.at[me],
                 send_sem=send,
                 recv_sem=recv,
-                device_id={axis: lax.rem(me + d, count)},
+                device_id={axis: peer},
                 device_id_type=MESH,
             ).start()
-            return carry
-
-        lax.fori_loop(1, count, one, 0)
 
     def whole(buf, count, axis, me, send, recv):
         part = buf.at[pl.ds(0, count - 1)]
@@ -226,87 +224,87 @@
         g_ref[:, cols] = ysq[:, cols] - (0.5 * LN2) * column_lse
         yr[extra, cols] = term_rows(LOG2E * tm_ref[:, cols] - tgt_base - column_lse)
 
-    def send_piece(d, first):
-        p = first + d
-
-        @pl.when(p != t)
-        def _():
-            pltpu.make_async_remote_copy(
-                src_ref=vals.at[lax.rem(p, 2), :, pl.ds(column_of(p), width)],
-                dst_ref=pieces.at[t],
-                send_sem=vsend,
-                recv_sem=vrecv,
-                device_id={"tgt": p},
-                device_id_type=MESH,
-            ).start()
-
-        return first
-
-    def column_of(p):
-        return pl.multiple_of((p // 2) * width, width)
-
-    owners = n_tgt // CHUNKS
-    for turn in (2, 1, 3, 0):
-        c = lax.rem(t // owners + turn, CHUNKS)
-        at = pl.ds(pl.multiple_of(c * chunk, chunk), chunk)
-        block = scores(yr[...], xr[:, at])
-        top = jnp.max(block, axis=0, keepdims=True)
-        weights = jnp.exp2(block - top)
-        total = jnp.sum(weights, axis=0, keepdims=True)
-        summed = lax.dot_general(
-            y_ref[...],
-            weights.astype(jnp.bfloat16),
-            (((1,), (0,)), ((), ())),
-            preferred_element_type=jnp.float32,
-        )
-        mean = summed / total
-        lse = jnp.broadcast_to(top + jnp.log2(total), (8, chunk))
-        for k in range(2):
-            vals[k, 0:half, at] = mean[k * half : (k + 1) * half]
-            vals[k, half : half + 8, at] = lse
-        lax.fori_loop(0, owners, send_piece, c * owners)
-
-    pieces[t] = vals[lax.rem(t, 2), :, pl.ds(column_of(t), width)]
-    whole(pieces, n_tgt, "tgt", t, vsend, vrecv).wait_recv()
-    lse = pieces[:, half : half + 1, :]
-    top = jnp.max(lse, axis=0, keepdims=True)
-    share = jnp.exp2(lse - top)
-    image = jnp.sum(pieces[:, 0:half, :] * share, axis=0) / jnp.sum(share, axis=0)
-    spot = (pl.ds(pl.multiple_of(lax.rem(t, 2) * half, half), half), pl.ds(column_of(t), width))
-    out_ref[spot] = image
-
-    def send_image(d, carry):
-        pltpu.make_async_remote_copy(
-            src_ref=out_ref.at[spot],
-            dst_ref=out_ref.at[spot],
-            send_sem=osend,
-            recv_sem=orecv,
-            device_id={"tgt": lax.rem(t + d, n_tgt)},
-            device_id_type=MESH,
-        ).start()
-        return carry
-
-    lax.fori_loop(1, n_tgt, send_image, 0)
-
-    def all_images():
-        part = pieces.at[pl.ds(0, n_tgt - 1), 0:half, :]
+    def place(phase, p):
+        return pl.multiple_of(phase * (rows // PHASES) + p // groups * width, width)
+
+    for phase in range(PHASES):
+        for turn in range(2):
+            k = lax.rem(t // (n_tgt // 2) + 1 + turn, 2)
+            at = pl.ds(pl.multiple_of((2 * phase + k) * chunk, chunk), chunk)
+            block = scores(yr[...], xr[:, at])
+            top = jnp.max(block, axis=0, keepdims=True)
+            weights = jnp.exp2(block - top)
+            total = jnp.sum(weights, axis=0, keepdims=True)
+            summed = lax.dot_general(
+                y_ref[...],
+                weights.astype(jnp.bfloat16),
+                (((1,), (0,)), ((), ())),
+                preferred_element_type=jnp.float32,
+            )
+            mean = summed / total
+            for q in range(groups):
+                vals[q, :, at] = mean[q * 8 : (q + 1) * 8]
+            logs[:, at] = top + jnp.log2(total)
+            near = [2 * ny * k + ny * r for r in (1 - lax.rem(t // ny, 2), lax.rem(t // ny, 2))]
+            owners = [b + a for a in ys for b in near]
+            for p in owners[:-1] if turn == 1 else owners:
+                lanes = pl.ds(place(phase, p), width)
+                for source, target, send, recv in (
+                    (vals.at[lax.rem(p, groups), :, lanes], pieces, vsend, vrecv),
+                    (logs.at[:, lanes], shares, lsend, lrecv),
+                ):
+                    pltpu.make_async_remote_copy(
+                        src_ref=source,
+                        dst_ref=target.at[phase, t],
+                        send_sem=send.at[phase],
+                        recv_sem=recv.at[phase],
+                        device_id={"tgt": p},
+                        device_id_type=MESH,
+                    ).start()
+
+    def all_pieces(phase, ref, send, recv):
+        part = ref.at[phase, pl.ds(0, n_tgt - 1)]
         return pltpu.make_async_remote_copy(
             src_ref=part,
             dst_ref=part,
-            send_sem=osend,
-            recv_sem=orecv,
-            device_id={"tgt": lax.rem(t + 1, n_tgt)},
+            send_sem=send.at[phase],
+            recv_sem=recv.at[phase],
+            device_id={"tgt": tgt_peers[0]},
             device_id_type=MESH,
         )
+
+    for phase in range(PHASES):
+        pieces[phase, t] = vals[lax.rem(t, groups), :, pl.ds(place(phase, t), width)]
+        shares[phase, t] = logs[:, pl.ds(place(phase, t), width)]
+        all_pieces(phase, shares, lsend, lrecv).wait_recv()
+        lse = shares[phase]
+        top = jnp.max(lse, axis=0, keepdims=True)
+        share = jnp.exp2(lse - top)
+        share = share / jnp.sum(share, axis=0, keepdims=True)
+        all_pieces(phase, pieces, vsend, vrecv).wait_recv()
+        image = jnp.sum(pieces[phase] * share, axis=0)
+        spot = (pl.ds(pl.multiple_of(lax.rem(t, groups) * 8, 8), 8), pl.ds(place(phase, t), width))
+        out_ref[spot] = image
+        for peer in tgt_peers:
+            pltpu.make_async_remote_copy(
+                src_ref=out_ref.at[spot],
+                dst_ref=out_ref.at[spot],
+                send_sem=osend.at[phase],
+                recv_sem=orecv.at[phase],
+                device_id={"tgt": peer},
+                device_id_type=MESH,
+            ).start()
 
     for iteration in range(ITERS):
         for c in range(CHUNKS):
             f_all(iteration, c).wait_send()
         for h in range(HALVES):
             g_all(iteration, h).wait_send()
-    whole(pieces, n_tgt, "tgt", t, vsend, vrecv).wait_send()
-    all_images().wait_recv()
-    all_images().wait_send()
+    for phase in range(PHASES):
+        all_pieces(phase, shares, lsend, lrecv).wait_send()
+        all_pieces(phase, pieces, vsend, vrecv).wait_send()
+        all_pieces(phase, pieces, osend, orecv).wait_recv()
+        all_pieces(phase, pieces, osend, orecv).wait_send()
 
 
 def store(f_in, g_in, out_in, f_out, g_out, out_out, sems):
@@ -361,17 +359,21 @@
                 pltpu.VMEM((8, columns), f32),
                 pltpu.VMEM((ITERS, CHUNKS, n_tgt, 1, chunk), f32),
                 pltpu.VMEM((ITERS, HALVES, n_src, 1, span), f32),
-                pltpu.VMEM((2, dim // 2 + 8, rows), f32),
-                pltpu.VMEM((n_tgt, dim // 2 + 8, 2 * rows // n_tgt), f32),
+                pltpu.VMEM((dim // 8, 8, rows), f32),
+                pltpu.VMEM((1, rows), f32),
+                pltpu.VMEM((PHASES, n_tgt, 8, dim // 8 * rows // (PHASES * n_tgt)), f32),
+                pltpu.VMEM((PHASES, n_tgt, 1, dim // 8 * rows // (PHASES * n_tgt)), f32),
                 dma((5,)),
                 dma((ITERS, CHUNKS)),
                 dma((ITERS, CHUNKS)),
                 dma((ITERS, HALVES)),
                 dma((ITERS, HALVES)),
-                dma,
-                dma,
-                dma,
-                dma,
+                dma((PHASES,)),
+                dma((PHASES,)),
+                dma((PHASES,)),
+                dma((PHASES,)),
+                dma((PHASES,)),
+                dma((PHASES,)),
             ],
             compiler_params=pltpu.CompilerParams(
                 collective_id=0, has_side_effects=True, vmem_limit_bytes=48 << 20

time: 71.5 us -> 65.3 us (0.913)
  Pallas kernels: 70.1 us -> 64.3 us
    pallas_call x1, Pallas kernels: 69.4 us -> 63.6 us  [local(): pl.pallas_call(functools.partial(kernel, n_src, n_tgt, math.log2(rows * n...]
where the time goes in v3:
time: 65.3 us; the launch traced here: 65.1 us
  Pallas kernels  64.3 us (98%)
  between operations  0.8 us (1%)
    pallas_call x1, Pallas kernels, local(): pl.pallas_call(functools.partial(kernel, n_src, n_tgt, math.log2(rows * n...  63.6 us

profile of v3, /device:TPU:6, one launch (start us, length us, event | category | flops | bytes accessed | tf_op | source)
XLA Modules:
  0.0 65.1 jit_solution(11241879658943537021)
XLA Ops:
  0.6 63.6 %shard_map.76 = (f32[1,2048]{1,0:T(1,128)S(1)}, f32[1,1024]{1,0:T(1,128)S(1)}, f32[32,2048]{1,0:T(8,128)S(1)}) custom-call(bf16[32,2048]{1,0:T(8,128)(2,1)} %x_hbm.1, bf16[32,1024]{1,0:T(8,128)(2,1)} %y_hbm.1, f32[1,2048]{1,0:T(1,128)} %bitcast.5, f32[1,1024]{1,0:T(1,128)} %bitcast.6, f32[1,1024]{1,0:T(1,128)} %bitcast.7), custom_call_target="tpu_custom_call" | custom-call | tf_op jit(solution)/shard_map/pallas_call | solution.py:337
  64.2 0.7 %shard_map.77 = (f32[1,2048]{1,0:T(1,128)}, f32[1,1024]{1,0:T(1,128)}, f32[32,2048]{1,0:T(8,128)}) custom-call(f32[1,2048]{1,0:T(1,128)S(1)} %get-tuple-element.9.f_in, f32[1,1024]{1,0:T(1,128)S(1)} %get-tuple-element.10.g_in, f32[32,2048]{1,0:T(8,128)S(1)} %get-tuple-element.11.out_in), custom_call_target="tpu_custom_call" | custom-call | tf_op jit(solution)/shard_map/pallas_call | solution.py:384

commit v4 on v3

--- a/solution.py
+++ b/solution.py
@@ -13,9 +13,11 @@
 LOG2E = math.log2(math.e)
 LN2 = math.log(2.0)
 DEPTH = 128
-CHUNKS = 4
+CHUNKS = 2
 HALVES = 1
 PHASES = 2
+MAPS = 4
+TILE = 256
 
 
 def far_first(n):
@@ -58,6 +60,18 @@
     groups = block.reshape(block.shape[0] // 8, 8, n)
     top = jnp.max(groups, axis=0)
     return top, jnp.sum(jnp.exp2(groups - top[None]), axis=0)
+
+
+def tiled(left, right, kept, reduced):
+    tops, sums = [], []
+    for a in range(kept.start, kept.stop, TILE):
+        pair = None
+        for b in range(reduced.start, reduced.stop, TILE):
+            piece = partial(scores(left[:, b : b + TILE], right[:, a : a + TILE]))
+            pair = piece if pair is None else merge(pair, piece)
+        tops.append(pair[0])
+        sums.append(pair[1])
+    return jnp.concatenate(tops, axis=1), jnp.concatenate(sums, axis=1)
 
 
 def merge(first, second):
@@ -177,7 +191,7 @@
             yr[extra, cols] = term_rows(terms)
             for c in range(CHUNKS):
                 at = slice(c * chunk, (c + 1) * chunk)
-                pair = partial(scores(yr[:, cols], xr[:, at]))
+                pair = tiled(yr, xr, at, cols)
                 if h > 0:
                     pair = merge((rtop[:, at], rsum[:, at]), pair)
                 if h < HALVES - 1:
@@ -205,7 +219,7 @@
             xc[extra, at] = term_rows(LOG2E * sm_ref[:, at] - src_base - row_lse)
             for h in range(HALVES):
                 cols = slice(h * span, (h + 1) * span)
-                pair = partial(scores(xc[:, at], yc[:, cols]))
+                pair = tiled(xc, yc, cols, at)
                 if c > 0:
                     pair = merge((ctop[:, cols], csum[:, cols]), pair)
                 if c < CHUNKS - 1:
@@ -227,10 +241,11 @@
     def place(phase, p):
         return pl.multiple_of(phase * (rows // PHASES) + p // groups * width, width)
 
+    piece = rows // MAPS
     for phase in range(PHASES):
         for turn in range(2):
             k = lax.rem(t // (n_tgt // 2) + 1 + turn, 2)
-            at = pl.ds(pl.multiple_of((2 * phase + k) * chunk, chunk), chunk)
+            at = pl.ds(pl.multiple_of((2 * phase + k) * piece, piece), piece)
             block = scores(yr[...], xr[:, at])
             top = jnp.max(block, axis=0, keepdims=True)
             weights = jnp.exp2(block - top)

time: 65.3 us -> 64.2 us (0.983)
  Pallas kernels: 64.3 us -> 63 us
    pallas_call x1, Pallas kernels: 63.6 us -> 62.2 us  [local(): pl.pallas_call(functools.partial(kernel, n_src, n_tgt, math.log2(rows * n...]
where the time goes in v4:
time: 64.2 us; the launch traced here: 63.6 us
  Pallas kernels  63 us (98%)
    pallas_call x1, Pallas kernels, local(): pl.pallas_call(functools.partial(kernel, n_src, n_tgt, math.log2(rows * n...  62.2 us

profile of v4, /device:TPU:6, one launch (start us, length us, event | category | flops | bytes accessed | tf_op | source)
XLA Modules:
  0.0 63.6 jit_solution(17249960234378703542)
XLA Ops:
  0.6 62.2 %shard_map.76 = (f32[1,2048]{1,0:T(1,128)S(1)}, f32[1,1024]{1,0:T(1,128)S(1)}, f32[32,2048]{1,0:T(8,128)S(1)}) custom-call(bf16[32,2048]{1,0:T(8,128)(2,1)} %x_hbm.1, bf16[32,1024]{1,0:T(8,128)(2,1)} %y_hbm.1, f32[1,2048]{1,0:T(1,128)} %bitcast.5, f32[1,1024]{1,0:T(1,128)} %bitcast.6, f32[1,1024]{1,0:T(1,128)} %bitcast.7), custom_call_target="tpu_custom_call" | custom-call | tf_op jit(solution)/shard_map/pallas_call | solution.py:352
  62.9 0.7 %shard_map.77 = (f32[1,2048]{1,0:T(1,128)}, f32[1,1024]{1,0:T(1,128)}, f32[32,2048]{1,0:T(8,128)}) custom-call(f32[1,2048]{1,0:T(1,128)S(1)} %get-tuple-element.9.f_in, f32[1,1024]{1,0:T(1,128)S(1)} %get-tuple-element.10.g_in, f32[32,2048]{1,0:T(8,128)S(1)} %get-tuple-element.11.out_in), custom_call_target="tpu_custom_call" | custom-call | tf_op jit(solution)/shard_map/pallas_call | solution.py:399

commit v5 on v4

--- a/solution.py
+++ b/solution.py
@@ -113,9 +113,6 @@
             )
         )
     ]
-    for copy in copies:
-        copy.start()
-
     nx, ny, nz = 4, n_tgt // 4, n_src // 2
     xs = [lax.rem(t // ny + d, nx) * ny for d in far_first(nx)]
     ys = [lax.rem(lax.rem(t, ny) + d, ny) for d in far_first(ny)]
@@ -128,6 +125,8 @@
     for axis, peers in (("tgt", tgt_peers), ("src", src_peers)):
         for peer in peers:
             pl.semaphore_signal(barrier, inc=1, device_id={axis: peer}, device_id_type=MESH)
+    for copy in copies:
+        copy.start()
     for copy in copies:
         copy.wait()
 
@@ -205,11 +204,16 @@
                         )
         if iteration == 0:
             pl.semaphore_wait(barrier, n_src + n_tgt - 2)
-            for c in range(CHUNKS):
-                send_all(
-                    fbuf.at[iteration, c], t, "tgt", n_tgt,
-                    fsend.at[iteration, c], frecv.at[iteration, c],
-                )
+            for peer in tgt_peers:
+                for c in range(CHUNKS):
+                    pltpu.make_async_remote_copy(
+                        src_ref=fbuf.at[iteration, c, t],
+                        dst_ref=fbuf.at[iteration, c, t],
+                        send_sem=fsend.at[iteration, c],
+                        recv_sem=frecv.at[iteration, c],
+                        device_id={"tgt": peer},
+                        device_id_type=MESH,
+                    ).start()
         for c in range(CHUNKS):
             at = slice(c * chunk, (c + 1) * chunk)
             f_all(iteration, c).wait_recv()

time: 64.2 us -> 64.9 us (1.011)
    pallas_call x1, Pallas kernels: 62.2 us -> 62.9 us  [local(): pl.pallas_call(functools.partial(kernel, n_src, n_tgt, math.log2(rows * n...]
where the time goes in v5:
time: 64.9 us; the launch traced here: 64.3 us
  Pallas kernels  63.6 us (98%)
    pallas_call x1, Pallas kernels, local(): pl.pallas_call(functools.partial(kernel, n_src, n_tgt, math.log2(rows * n...  62.9 us

profile of v5, /device:TPU:6, one launch (start us, length us, event | category | flops | bytes accessed | tf_op | source)
XLA Modules:
  0.0 64.3 jit_solution(3784395828857206290)
XLA Ops:
  0.6 62.9 %shard_map.76 = (f32[1,2048]{1,0:T(1,128)S(1)}, f32[1,1024]{1,0:T(1,128)S(1)}, f32[32,2048]{1,0:T(8,128)S(1)}) custom-call(bf16[32,2048]{1,0:T(8,128)(2,1)} %x_hbm.1, bf16[32,1024]{1,0:T(8,128)(2,1)} %y_hbm.1, f32[1,2048]{1,0:T(1,128)} %bitcast.5, f32[1,1024]{1,0:T(1,128)} %bitcast.6, f32[1,1024]{1,0:T(1,128)} %bitcast.7), custom_call_target="tpu_custom_call" | custom-call | tf_op jit(solution)/shard_map/pallas_call | solution.py:356
  63.6 0.7 %shard_map.77 = (f32[1,2048]{1,0:T(1,128)}, f32[1,1024]{1,0:T(1,128)}, f32[32,2048]{1,0:T(8,128)}) custom-call(f32[1,2048]{1,0:T(1,128)S(1)} %get-tuple-element.9.f_in, f32[1,1024]{1,0:T(1,128)S(1)} %get-tuple-element.10.g_in, f32[32,2048]{1,0:T(8,128)S(1)} %get-tuple-element.11.out_in), custom_call_target="tpu_custom_call" | custom-call | tf_op jit(solution)/shard_map/pallas_call | solution.py:403
